TPU v7x, 32 devices: a whole 2x2x4 slice. The times are simulated.
32 devices in a mesh: row: 8 (over y, x, core), ka: 4 (over z).
Axes of the slice: x: 2, y: 2, z: 4, core: 2. Of those that a mesh axis runs over, the one named last changes fastest.
Arguments:
- pair_rep: bfloat16 [32, 32, 128], P('row', 'ka'), may hold values from -6 to 6
- in_weights: bfloat16 [2, 128, 512], replicated, may hold values from -0.5 to 0.5
- gate_weights: bfloat16 [2, 128, 128], replicated, may hold values from -0.5 to 0.5
- out_weights: bfloat16 [2, 128, 128], replicated, may hold values from -0.5 to 0.5
Outputs:
- refined: bfloat16 [32, 32, 128], P('row', 'ka')
All inputs are finite; a program needn't handle non-finite values.
Results may differ from a plain program's by a relative error of at most 0.015.
Values may be sent and summed in bfloat16 or wider, within the bound.
A program may use at most 64 MiB of HBM per device.

v0:
```python
import jax
import jax.numpy as jnp
from jax import lax
from jax.sharding import PartitionSpec as P

EPSILON = 1e-05


def normalize(values):
    values = values.astype(jnp.float32)
    centre = jnp.mean(values, axis=-1, keepdims=True)
    shifted = values - centre
    spread = jnp.mean(shifted * shifted, axis=-1, keepdims=True)
    return shifted * lax.rsqrt(spread + EPSILON)


def flatten_normed(blocks):
    normed = normalize(blocks).astype(jnp.bfloat16)
    return normed.reshape(-1, blocks.shape[-1])


def operands(flattened, weights, shape):
    columns = weights.shape[1] // 4
    projected = jnp.dot(flattened, weights, preferred_element_type=jnp.float32)
    left_rows = (
        jax.nn.sigmoid(projected[:, :columns]) * projected[:, columns : 2 * columns]
    ).astype(jnp.bfloat16)
    right_rows = (
        jax.nn.sigmoid(projected[:, 2 * columns : 3 * columns]) * projected[:, 3 * columns :]
    ).astype(jnp.bfloat16)
    return (
        left_rows.reshape(shape[0], shape[1], columns),
        right_rows.reshape(shape[0], shape[1], columns),
    )


def gates(flattened, weights, shape):
    gating = jax.nn.sigmoid(jnp.dot(flattened, weights, preferred_element_type=jnp.float32))
    return gating.reshape(shape[0], shape[1], weights.shape[1])


def triangle(left_rows, right_rows):
    partial_value = jnp.einsum(
        "ikh,jkh->ijh",
        left_rows,
        lax.all_gather(right_rows, "row", axis=0, tiled=True),
        preferred_element_type=jnp.float32,
    )
    return lax.psum_scatter(
        partial_value.astype(jnp.bfloat16), "ka", scatter_dimension=1, tiled=True
    ).astype(jnp.float32)


def finish(state, gating, product, weights):
    squeezed = normalize(product).astype(jnp.bfloat16).reshape(-1, product.shape[-1])
    update = jnp.dot(squeezed, weights, preferred_element_type=jnp.float32).reshape(gating.shape)
    return (state.astype(jnp.float32) + gating * update).astype(jnp.bfloat16)


def per_device(pair_rep, in_weights, gate_weights, out_weights):
    shape = pair_rep.shape
    flattened = flatten_normed(pair_rep)
    left_rows, right_rows = operands(flattened, in_weights[0], shape)
    gating = gates(flattened, gate_weights[0], shape)
    middle = finish(pair_rep, gating, triangle(left_rows, right_rows), out_weights[0])
    arrived = lax.all_to_all(
        jnp.swapaxes(middle, 0, 1), "ka", split_axis=1, concat_axis=0, tiled=True
    )
    arrived = lax.all_to_all(arrived, "row", split_axis=0, concat_axis=1, tiled=True)
    left_far, right_far = operands(flatten_normed(arrived), in_weights[1], arrived.shape)
    gating_far = gates(flatten_normed(middle), gate_weights[1], shape)
    return finish(middle, gating_far, triangle(left_far, right_far), out_weights[1])


def solution(mesh):
    in_specs = (P("row", "ka", None), P(), P(), P())
    out_specs = P("row", "ka", None)
    return jax.shard_map(
        per_device, mesh=mesh, in_specs=in_specs, out_specs=out_specs, check_vma=False
    )
```

profile of v0, /device:TPU:0, one launch (start us, length us, event | category | flops | bytes accessed | tf_op | source)
XLA Modules:
  0.0 86.3 jit_solution(1620669610929316636)
XLA Ops:
  0.0 0.9 convert_reduce_fusion.1
  1.0 1.1 %fusion.16 = f32[32,512]{1,0:T(8,128)S(1)} fusion(bf16[2,128,512]{2,1,0:T(8,128)(2,1)} %param.5, bf16[4,8,128]{2,1,0:T(8,128)(2,1)S(1)} %copy-done.1, f32[4,8]{1,0:T(4,128)S(1)} %add_rsqrt_fusion.4, f32[4,8]{1,0:T(4,128)S(1)} %broadcast_multiply_fusion.4), kind=kOutput, calls=%fused_computation.22 | convolution fusion | flops 4210688 | bytes 205056 | tf_op jit(solution)/shard_map/dot_general | solution.py:24
  2.2 10.7 %all_gather.6 = bf16[32,8,128]{2,1,0:T(8,128)(2,1)S(1)} all-gather(bf16[4,8,128]{2,1,0:T(8,128)(2,1)S(1)} %get-tuple-element.8), channel_id=1, replica_groups=mesh['row'=8,'ka'=4] {'row'}, dimensions={0}, use_global_device_ids=true | all-gather | bytes 73728 | tf_op jit(solution)/shard_map/all_gather | solution.py:46
  12.9 1.4 %copy.65 = bf16[32,8,128]{1,0,2:T(8,128)(2,1)S(1)} copy(bf16[32,8,128]{2,1,0:T(8,128)(2,1)S(1)} %all_gather.6) | data formatting | bytes 131072 | tf_op jit(solution)/shard_map/all_gather | solution.py:46
  14.5 0.6 fusion
  15.3 19.4 %all-reduce = bf16[4,32,128]{2,0,1:T(4,128)(2,1)S(1)} all-reduce(bf16[4,32,128]{2,0,1:T(4,128)(2,1)S(1)} %copy.67), channel_id=2, replica_groups=mesh['row'=8,'ka'=4] {'ka'}, use_global_device_ids=true, to_apply=%region_2.0.clone | all-reduce | flops 16384 | bytes 65536
  34.7 0.6 copy-done.4
  35.3 0.6 dynamic-slice
  37.2 0.4 copy-done.2
  37.5 0.7 convert_reduce_fusion
  38.3 3.2 %all-to-all-start = ((bf16[8,4,128]{2,0,1:T(8,128)(2,1)}), bf16[8,4,128]{2,0,1:T(8,128)(2,1)S(1)}, u32[]{:S(2)}, u32[]{:S(2)}) async-start(bf16[8,4,128]{2,0,1:T(8,128)(2,1)} %bitcast.12), calls=%async_computation | async-start | bytes 16384 | tf_op jit(solution)/shard_map/all_to_all | solution.py:66
  41.5 0.9 %fusion.42 = f32[4,8]{1,0:T(4,128)S(1)} fusion(bf16[4,8,128]{2,1,0:T(8,128)(2,1)} %get-tuple-element.10, f32[4,8]{1,0:T(4,128)S(1)} %broadcast_multiply_fusion.3), kind=kLoop, calls=%fused_computation.58 | loop fusion | flops 16352 | bytes 8448 | tf_op jit(solution)/shard_map/reduce_sum | solution.py:13
  42.4 4.6 %all-to-all-done = bf16[8,4,128]{2,0,1:T(8,128)(2,1)S(1)} async-done(((bf16[8,4,128]{2,0,1:T(8,128)(2,1)}), bf16[8,4,128]{2,0,1:T(8,128)(2,1)S(1)}, u32[]{:S(2)}, u32[]{:S(2)}) %all-to-all-start) | async-done | bytes 8224 | tf_op jit(solution)/shard_map/all_to_all | solution.py:66
  47.1 0.6 broadcast.145
  47.7 0.7 reduce.1
  48.4 0.6 reshape.129
  49.0 3.3 %all-to-all-start.1 = ((bf16[8,2,256]{2,1,0:T(2,128)(2,1)}), bf16[8,2,256]{2,1,0:T(2,128)(2,1)S(1)}, u32[]{:S(2)}, u32[]{:S(2)}) async-start(bf16[8,2,256]{2,1,0:T(2,128)(2,1)} %reshape.129), calls=%async_computation.1 | async-start | bytes 16384 | tf_op jit(solution)/shard_map/all_to_all | solution.py:69
  52.3 0.9 %fusion.6 = f32[4,8,128]{2,1,0:T(8,128)S(1)} fusion(bf16[2,128,128]{2,1,0:T(8,128)(2,1)S(1)} %copy-done.3, bf16[4,8,128]{2,1,0:T(8,128)(2,1)} %get-tuple-element.10, f32[4,8]{1,0:T(4,128)S(1)} %add_rsqrt_fusion.3, f32[4,8]{1,0:T(4,128)S(1)} %broadcast_multiply_fusion.3), kind=kOutput, calls=%fused_computation.10 | convolution fusion | flops 1077248 | bytes 61440 | tf_op jit(solution)/shard_map/dot_general | solution.py:38
  53.2 3.7 %all-to-all-done.1 = bf16[8,2,256]{2,1,0:T(2,128)(2,1)S(1)} async-done(((bf16[8,2,256]{2,1,0:T(2,128)(2,1)}), bf16[8,2,256]{2,1,0:T(2,128)(2,1)S(1)}, u32[]{:S(2)}, u32[]{:S(2)}) %all-to-all-start.1) | async-done | bytes 8224 | tf_op jit(solution)/shard_map/all_to_all | solution.py:69
  57.5 8.3 %all_gather.7 = bf16[32,8,128]{2,1,0:T(8,128)(2,1)S(1)} all-gather(bf16[4,8,128]{2,1,0:T(8,128)(2,1)S(1)} %get-tuple-element.6), channel_id=1, replica_groups=mesh['row'=8,'ka'=4] {'row'}, dimensions={0}, use_global_device_ids=true | all-gather | bytes 73728 | tf_op jit(solution)/shard_map/all_gather | solution.py:46
  65.8 1.4 %copy.81 = bf16[32,8,128]{1,0,2:T(8,128)(2,1)S(1)} copy(bf16[32,8,128]{2,1,0:T(8,128)(2,1)S(1)} %all_gather.7) | data formatting | bytes 131072 | tf_op jit(solution)/shard_map/all_gather | solution.py:46
  67.4 0.6 fusion.1
  68.2 16.3 %all-reduce.1 = bf16[4,32,128]{2,0,1:T(4,128)(2,1)S(1)} all-reduce(bf16[4,32,128]{2,0,1:T(4,128)(2,1)S(1)} %copy.83), channel_id=3, replica_groups=mesh['row'=8,'ka'=4] {'ka'}, use_global_device_ids=true, to_apply=%region_9.0.clone | all-reduce | flops 16384 | bytes 65536
  84.8 1.4 %fusion.13 = bf16[4,8,128]{2,1,0:T(8,128)(2,1)} fusion(f32[4,8,128]{2,1,0:T(8,128)S(1)} %fusion.6, bf16[2,128,128]{2,1,0:T(8,128)(2,1)S(1)} %copy-done.2, bf16[4,8,128]{2,1,0:T(8,128)(2,1)} %get-tuple-element.10, bf16[4,8,128]{2,0,1:T(4,128)(2,1)S(1)} %fusion.39), kind=kOutput, calls=%fused_computation.19 | convolution fusion | flops 1064960 | bytes 73728 | tf_op jit(solution)/shard_map/dot_general | solution.py:56
  (38 shorter events, 2.2 us)
Async XLA Ops:
  0.0 0.9 %copy-start.1 = (bf16[4,8,128]{2,1,0:T(8,128)(2,1)S(1)}, bf16[4,8,128]{2,1,0:T(8,128)(2,1)}, u32[]{:S(2)}) copy-start(bf16[4,8,128]{2,1,0:T(8,128)(2,1)} %param.4) | copy-start | bytes 24580
  15.3 21.7 %copy-start.3 = (bf16[2,128,128]{2,1,0:T(8,128)(2,1)S(1)}, bf16[2,128,128]{2,1,0:T(8,128)(2,1)}, u32[]{:S(2)}) copy-start(bf16[2,128,128]{2,1,0:T(8,128)(2,1)} %param.6) | copy-start | bytes 196612
  34.7 0.7 copy-start.4
  36.7 0.8 copy-start.2
  37.0 20.4 %copy-start = (bf16[2,128,512]{2,1,0:T(8,128)(2,1)S(1)}, bf16[2,128,512]{2,1,0:T(8,128)(2,1)}, u32[]{:S(2)}) copy-start(bf16[2,128,512]{2,1,0:T(8,128)(2,1)} %param.5) | copy-start | bytes 786436
  38.3 8.8 %all-to-all-start = ((bf16[8,4,128]{2,0,1:T(8,128)(2,1)}), bf16[8,4,128]{2,0,1:T(8,128)(2,1)S(1)}, u32[]{:S(2)}, u32[]{:S(2)}) async-start(bf16[8,4,128]{2,0,1:T(8,128)(2,1)} %bitcast.12), calls=%async_computation | async-start | bytes 16384 | tf_op jit(solution)/shard_map/all_to_all | solution.py:66
  49.0 8.0 %all-to-all-start.1 = ((bf16[8,2,256]{2,1,0:T(2,128)(2,1)}), bf16[8,2,256]{2,1,0:T(2,128)(2,1)S(1)}, u32[]{:S(2)}, u32[]{:S(2)}) async-start(bf16[8,2,256]{2,1,0:T(2,128)(2,1)} %reshape.129), calls=%async_computation.1 | async-start | bytes 16384 | tf_op jit(solution)/shard_map/all_to_all | solution.py:69
where the time goes:
time: 86.9 us; the launch traced here: 86.3 us
  blocking collectives  54.7 us (63%)
  waiting for transfers between devices  8.39 us (10%)
  starting transfers between devices  6.58 us (8%)
  local copies, waits for them, and re-layouts  6.25 us (7%)
  matrix products  5.78 us (7%)
  other arithmetic  3.7 us (4%)
  between operations  0.88 us (1%)
    unnamed x2, blocking collectives  35.7 us
    all_gather x2, blocking collectives, triangle(): lax.all_gather(right_rows, 'row', axis=0, tiled=True)  19 us
    all_to_all x1, waiting for transfers between devices, per_device(): lax.all_to_all(jnp.swapaxes(middle, 0, 1), 'ka', split_axis=1, concat_axi...  4.65 us
    all_to_all x1, waiting for transfers between devices, per_device(): lax.all_to_all(arrived, 'row', split_axis=0, concat_axis=1, tiled=True)  3.74 us
    all_to_all x1, starting transfers between devices, per_device(): lax.all_to_all(arrived, 'row', split_axis=0, concat_axis=1, tiled=True)  3.33 us
    all_to_all x1, starting transfers between devices, per_device(): lax.all_to_all(jnp.swapaxes(middle, 0, 1), 'ka', split_axis=1, concat_axi...  3.25 us
    all_gather x2, local copies, waits for them, and re-layouts, triangle(): lax.all_gather(right_rows, 'row', axis=0, tiled=True)  2.86 us
    unnamed x13, local copies, waits for them, and re-layouts  2.22 us
  transfers between devices with their start and end apart: 2, of which 2 were waited for; matrix products, arithmetic and copies ran while one was open for 2% of the time, Pallas kernels for 0%

commit v1 on v0

--- a/solution.py
+++ b/solution.py
@@ -66,7 +66,10 @@
     arrived = lax.all_to_all(
         jnp.swapaxes(middle, 0, 1), "ka", split_axis=1, concat_axis=0, tiled=True
     )
-    arrived = lax.all_to_all(arrived, "row", split_axis=0, concat_axis=1, tiled=True)
+    arrived = jnp.concatenate(
+        lax.all_to_all(jnp.stack(jnp.split(arrived, lax.axis_size("row"), axis=0)), "row", 0, 0),
+        axis=1,
+    )
     left_far, right_far = operands(flatten_normed(arrived), in_weights[1], arrived.shape)
     gating_far = gates(flatten_normed(middle), gate_weights[1], shape)
     return finish(middle, gating_far, triangle(left_far, right_far), out_weights[1])

time: 86.9 us -> 89.6 us (1.031)
  local copies, waits for them, and re-layouts: 6.25 us -> 9.69 us
    unnamed x13 -> x18, local copies, waits for them, and re-layouts: 2.22 us -> 5.68 us
where the time goes in v1:
time: 89.6 us; the launch traced here: 89 us
  blocking collectives  54.7 us (61%)
  local copies, waits for them, and re-layouts  9.69 us (11%)
  waiting for transfers between devices  8.39 us (9%)
  starting transfers between devices  6.58 us (7%)
  matrix products  5.78 us (6%)
  other arithmetic  3 us (3%)
    unnamed x2, blocking collectives  35.7 us
    all_gather x2, blocking collectives, triangle(): lax.all_gather(right_rows, 'row', axis=0, tiled=True)  19 us
    unnamed x18, local copies, waits for them, and re-layouts  5.68 us
    all_to_all x1, waiting for transfers between devices, per_device(): lax.all_to_all(jnp.swapaxes(middle, 0, 1), 'ka', split_axis=1, concat_axi...  4.65 us
    all_to_all x1, waiting for transfers between devices, per_device(): lax.all_to_all(jnp.stack(jnp.split(arrived, lax.axis_size('row'), axis=0)...  3.74 us
    all_to_all x1, starting transfers between devices, per_device(): lax.all_to_all(jnp.stack(jnp.split(arrived, lax.axis_size('row'), axis=0)...  3.33 us
    all_to_all x1, starting transfers between devices, per_device(): lax.all_to_all(jnp.swapaxes(middle, 0, 1), 'ka', split_axis=1, concat_axi...  3.25 us
    all_gather x2, local copies, waits for them, and re-layouts, triangle(): lax.all_gather(right_rows, 'row', axis=0, tiled=True)  2.86 us
  transfers between devices with their start and end apart: 2, of which 2 were waited for; matrix products, arithmetic and copies ran while one was open for 2% of the time, Pallas kernels for 0%

profile of v1, /device:TPU:0, one launch (start us, length us, event | category | flops | bytes accessed | tf_op | source)
XLA Modules:
  0.0 89.0 jit_solution(16018863513838881642)
XLA Ops:
  0.0 0.9 convert_reduce_fusion.1
  1.0 1.1 %fusion.16 = f32[32,512]{1,0:T(8,128)S(1)} fusion(bf16[2,128,512]{2,1,0:T(8,128)(2,1)} %param.5, bf16[4,8,128]{2,1,0:T(8,128)(2,1)S(1)} %copy-done.1, f32[4,8]{1,0:T(4,128)S(1)} %add_rsqrt_fusion.4, f32[4,8]{1,0:T(4,128)S(1)} %broadcast_multiply_fusion.4), kind=kOutput, calls=%fused_computation.22 | convolution fusion | flops 4210688 | bytes 205056 | tf_op jit(solution)/shard_map/dot_general | solution.py:24
  2.2 10.7 %all_gather.6 = bf16[32,8,128]{2,1,0:T(8,128)(2,1)S(1)} all-gather(bf16[4,8,128]{2,1,0:T(8,128)(2,1)S(1)} %get-tuple-element.8), channel_id=1, replica_groups=mesh['row'=8,'ka'=4] {'row'}, dimensions={0}, use_global_device_ids=true | all-gather | bytes 73728 | tf_op jit(solution)/shard_map/all_gather | solution.py:46
  12.9 1.4 %copy.68 = bf16[32,8,128]{1,0,2:T(8,128)(2,1)S(1)} copy(bf16[32,8,128]{2,1,0:T(8,128)(2,1)S(1)} %all_gather.6) | data formatting | bytes 131072 | tf_op jit(solution)/shard_map/all_gather | solution.py:46
  14.5 0.6 fusion
  15.3 19.4 %all-reduce = bf16[4,32,128]{2,0,1:T(4,128)(2,1)S(1)} all-reduce(bf16[4,32,128]{2,0,1:T(4,128)(2,1)S(1)} %copy.70), channel_id=2, replica_groups=mesh['row'=8,'ka'=4] {'ka'}, use_global_device_ids=true, to_apply=%region_2.0.clone | all-reduce | flops 16384 | bytes 65536
  34.7 0.6 copy-done.4
  35.3 0.6 dynamic-slice
  37.5 0.7 convert_reduce_fusion
  38.3 3.2 %all-to-all-start = ((bf16[8,4,128]{2,0,1:T(8,128)(2,1)}), bf16[8,4,128]{2,0,1:T(8,128)(2,1)S(1)}, u32[]{:S(2)}, u32[]{:S(2)}) async-start(bf16[8,4,128]{2,0,1:T(8,128)(2,1)} %bitcast.12), calls=%async_computation | async-start | bytes 16384 | tf_op jit(solution)/shard_map/all_to_all | solution.py:66
  41.5 0.9 fusion.42
  42.4 4.6 %all-to-all-done = bf16[8,4,128]{2,0,1:T(8,128)(2,1)S(1)} async-done(((bf16[8,4,128]{2,0,1:T(8,128)(2,1)}), bf16[8,4,128]{2,0,1:T(8,128)(2,1)S(1)}, u32[]{:S(2)}, u32[]{:S(2)}) %all-to-all-start) | async-done | bytes 8224 | tf_op jit(solution)/shard_map/all_to_all | solution.py:66
  47.1 0.6 constant_dynamic-update-slice_fusion.7
  47.7 0.6 constant_dynamic-update-slice_fusion.6
  49.4 0.6 constant_dynamic-update-slice_fusion.3
  51.1 0.6 constant_dynamic-update-slice_fusion
  51.7 3.3 %all-to-all-start.1 = ((bf16[8,4,1,128]{3,1,2,0:T(4,128)(2,1)}), bf16[8,4,1,128]{3,1,2,0:T(4,128)(2,1)S(1)}, u32[]{:S(2)}, u32[]{:S(2)}) async-start(bf16[8,4,1,128]{3,1,2,0:T(4,128)(2,1)} %constant_dynamic-update-slice_fusion), calls=%async_computation.1 | async-start | bytes 16384 | tf_op jit(solution)/shard_map/all_to_all | solution.py:70
  55.1 0.9 %fusion.6 = f32[4,8,128]{2,1,0:T(8,128)S(1)} fusion(bf16[2,128,128]{2,1,0:T(8,128)(2,1)S(1)} %copy-done.3, bf16[4,8,128]{2,1,0:T(8,128)(2,1)} %get-tuple-element.10, f32[4,8]{1,0:T(4,128)S(1)} %add_rsqrt_fusion.3, f32[4,8]{1,0:T(4,128)S(1)} %broadcast_multiply_fusion.3), kind=kOutput, calls=%fused_computation.10 | convolution fusion | flops 1077248 | bytes 61440 | tf_op jit(solution)/shard_map/dot_general | solution.py:38
  56.0 3.7 %all-to-all-done.1 = bf16[8,4,1,128]{3,1,2,0:T(4,128)(2,1)S(1)} async-done(((bf16[8,4,1,128]{3,1,2,0:T(4,128)(2,1)}), bf16[8,4,1,128]{3,1,2,0:T(4,128)(2,1)S(1)}, u32[]{:S(2)}, u32[]{:S(2)}) %all-to-all-start.1) | async-done | bytes 8224 | tf_op jit(solution)/shard_map/all_to_all | solution.py:70
  60.2 8.3 %all_gather.7 = bf16[32,8,128]{2,1,0:T(8,128)(2,1)S(1)} all-gather(bf16[4,8,128]{2,1,0:T(8,128)(2,1)S(1)} %get-tuple-element.6), channel_id=1, replica_groups=mesh['row'=8,'ka'=4] {'row'}, dimensions={0}, use_global_device_ids=true | all-gather | bytes 73728 | tf_op jit(solution)/shard_map/all_gather | solution.py:46
  68.5 1.4 %copy.82 = bf16[32,8,128]{1,0,2:T(8,128)(2,1)S(1)} copy(bf16[32,8,128]{2,1,0:T(8,128)(2,1)S(1)} %all_gather.7) | data formatting | bytes 131072 | tf_op jit(solution)/shard_map/all_gather | solution.py:46
  70.1 0.6 fusion.1
  70.9 16.3 %all-reduce.1 = bf16[4,32,128]{2,0,1:T(4,128)(2,1)S(1)} all-reduce(bf16[4,32,128]{2,0,1:T(4,128)(2,1)S(1)} %copy.84), channel_id=3, replica_groups=mesh['row'=8,'ka'=4] {'ka'}, use_global_device_ids=true, to_apply=%region_9.0.clone | all-reduce | flops 16384 | bytes 65536
  87.5 1.4 %fusion.13 = bf16[4,8,128]{2,1,0:T(8,128)(2,1)} fusion(f32[4,8,128]{2,1,0:T(8,128)S(1)} %fusion.6, bf16[2,128,128]{2,1,0:T(8,128)(2,1)S(1)} %copy-done.2, bf16[4,8,128]{2,1,0:T(8,128)(2,1)} %get-tuple-element.10, bf16[4,8,128]{2,0,1:T(4,128)(2,1)S(1)} %fusion.39), kind=kOutput, calls=%fused_computation.19 | convolution fusion | flops 1064960 | bytes 73728 | tf_op jit(solution)/shard_map/dot_general | solution.py:56
  (41 shorter events, 4.8 us)
Async XLA Ops:
  0.0 0.9 copy-start.1
  15.3 21.7 %copy-start.3 = (bf16[2,128,128]{2,1,0:T(8,128)(2,1)S(1)}, bf16[2,128,128]{2,1,0:T(8,128)(2,1)}, u32[]{:S(2)}) copy-start(bf16[2,128,128]{2,1,0:T(8,128)(2,1)} %param.6) | copy-start | bytes 196612
  34.7 0.7 copy-start.4
  36.7 0.8 copy-start.2
  36.8 23.2 %copy-start = (bf16[2,128,512]{2,1,0:T(8,128)(2,1)S(1)}, bf16[2,128,512]{2,1,0:T(8,128)(2,1)}, u32[]{:S(2)}) copy-start(bf16[2,128,512]{2,1,0:T(8,128)(2,1)} %param.5) | copy-start | bytes 786436
  38.3 8.8 %all-to-all-start = ((bf16[8,4,128]{2,0,1:T(8,128)(2,1)}), bf16[8,4,128]{2,0,1:T(8,128)(2,1)S(1)}, u32[]{:S(2)}, u32[]{:S(2)}) async-start(bf16[8,4,128]{2,0,1:T(8,128)(2,1)} %bitcast.12), calls=%async_computation | async-start | bytes 16384 | tf_op jit(solution)/shard_map/all_to_all | solution.py:66
  51.7 8.0 %all-to-all-start.1 = ((bf16[8,4,1,128]{3,1,2,0:T(4,128)(2,1)}), bf16[8,4,1,128]{3,1,2,0:T(4,128)(2,1)S(1)}, u32[]{:S(2)}, u32[]{:S(2)}) async-start(bf16[8,4,1,128]{3,1,2,0:T(4,128)(2,1)} %constant_dynamic-update-slice_fusion), calls=%async_computation.1 | async-start | bytes 16384 | tf_op jit(solution)/shard_map/all_to_all | solution.py:70
